TPU v7x, 32 devices: a whole 2x2x4 slice. The times are simulated.
32 devices in a mesh: gy: 4 (over x, core), gz: 2 (over y), ga: 4 (over z).
Axes of the slice: x: 2, y: 2, z: 4, core: 2. Of those that a mesh axis runs over, the one named last changes fastest.
Arguments:
- fields: float32 [16, 256, 8, 512], P(None, 'gy', 'gz', 'ga'), may hold values from -6 to 6
- section_start: float32 [16, 256, 8, 512], P(None, 'gy', 'gz', 'ga'), may hold values from -6 to 6
- velocity: float32 [3, 256, 8, 512], P(None, 'gy', 'gz', 'ga'), may hold values from -4 to 4
- diffusivity: float32 [16], replicated, may hold values from 0.02 to 0.2
- reaction: float32 [16, 16], replicated, may hold values from -1.5 to 1.5
- x_factor: bfloat16 [512, 64], replicated, may hold values from -0.25 to 0.25
- y_factor: float32 [256, 64], replicated, may hold values from -6 to 6
Outputs:
- new_fields: float32 [16, 256, 8, 512], P(None, 'gy', 'gz', 'ga')
- x_gram: float32 [512, 512], P(('gy', 'gz'))
- y_products: float32 [8, 256, 64], P(('gz', 'gy'))
All inputs are finite; a program needn't handle non-finite values.
Results may differ from a plain program's by a relative error of at most 0.0028.
Values may be sent and summed in bfloat16 or wider, within the bound.
No kernel may reach another device: no remote copies, remote signals or barrier semaphores. Data moves between devices by JAX's collectives and lax.ppermute only.
A program may use at most 64 MiB of HBM per device.

v0:
```python
import jax
import jax.numpy as jnp
from jax import lax
from jax.sharding import PartitionSpec as P

time_step = 0.4


def with_halo(block, sides, width):
    for axis, dim in sides:
        count = lax.axis_size(axis)
        forward = [(i, i + 1) for i in range(count - 1)]
        backward = [(target, source) for source, target in forward]
        low = lax.ppermute(
            lax.slice_in_dim(block, block.shape[dim] - width, None, axis=dim), axis, forward
        )
        high = lax.ppermute(lax.slice_in_dim(block, 0, width, axis=dim), axis, backward)
        block = jnp.concatenate([low, block, high], axis=dim)
    return block


def shards(fields, section_start, velocity, diffusivity, reaction, x_factor, y_factor):
    padded = with_halo(fields, (("gy", 1), ("gz", 2), ("ga", 3)), 1)
    center = padded[:, 1:-1, 1:-1, 1:-1]
    y_plus = padded[:, 2:, 1:-1, 1:-1]
    y_minus = padded[:, :-2, 1:-1, 1:-1]
    z_plus = padded[:, 1:-1, 2:, 1:-1]
    z_minus = padded[:, 1:-1, :-2, 1:-1]
    x_plus = padded[:, 1:-1, 1:-1, 2:]
    x_minus = padded[:, 1:-1, 1:-1, :-2]
    laplace_sum = y_plus + y_minus + z_plus + z_minus + x_plus + x_minus - 6.0 * center
    advection = (
        velocity[0][None] * (x_plus - x_minus) * 0.5
        + velocity[1][None] * (y_plus - y_minus) * 0.5
        + velocity[2][None] * (z_plus - z_minus) * 0.5
    )
    diffusion = diffusivity[:, None, None, None]
    tendency = (
        diffusion * laplace_sum
        - advection
        + jnp.einsum("vw,wyzx->vyzx", reaction, fields, precision=lax.Precision.HIGHEST)
    )
    section_value = 0.75 * section_start + 0.25 * (fields + time_step * tendency)
    buffer_rank = lax.axis_index("ga") == lax.axis_size("ga") - 1
    new_fields = jnp.where(buffer_rank, fields, section_value)
    snapshot = new_fields.astype(jnp.bfloat16)
    devices = lax.axis_size("gy") * lax.axis_size("gz")
    rank_x = x_factor.shape[1]
    gathered = lax.all_gather(snapshot, "ga", axis=3, tiled=True)
    variables, y_cells, z_cells, x_cells = gathered.shape
    unfolded = gathered.reshape(variables * y_cells * z_cells, x_cells)
    cell_count = float(variables * y_cells * z_cells * devices)
    gram_rows = lax.psum_scatter(
        lax.dot_general(
            unfolded, unfolded, (((0,), (0,)), ((), ())), preferred_element_type=jnp.float32
        ),
        ("gy", "gz"),
        scatter_dimension=0,
        tiled=True,
    )
    x_gram = gram_rows / cell_count
    projected = jnp.einsum(
        "vyzx,xr->yzvr", gathered, x_factor, preferred_element_type=jnp.float32
    ).astype(jnp.bfloat16)
    projected = projected.reshape(y_cells, z_cells, variables * rank_x)
    full_y = lax.all_to_all(projected, "gy", split_axis=1, concat_axis=0, tiled=True)
    y_gram = jnp.einsum("yzc,wzc->zyw", full_y, full_y, preferred_element_type=jnp.float32) / float(
        variables * rank_x
    )
    y_products = jnp.einsum("zyw,wk->zyk", y_gram, y_factor, precision=lax.Precision.HIGHEST)
    return (new_fields, x_gram, y_products)


def solution(mesh):
    in_specs = (
        P(None, "gy", "gz", "ga"),
        P(None, "gy", "gz", "ga"),
        P(None, "gy", "gz", "ga"),
        P(),
        P(),
        P(),
        P(),
    )
    out_specs = (P(None, "gy", "gz", "ga"), P(("gy", "gz"), None), P(("gz", "gy"), None, None))
    return jax.shard_map(shards, mesh=mesh, in_specs=in_specs, out_specs=out_specs, check_vma=False)
```

profile of v0, /device:TPU:0, one launch (start us, length us, event | category | flops | bytes accessed | tf_op | source)
XLA Modules:
  0.0 199.7 jit_solution(294682262062690017)
XLA Ops:
  7.2 3.0 %copy.52 = f32[16,64,4,128]{3,0,2,1:T(8,128)S(1)} copy(f32[16,64,4,128]{3,2,1,0:T(4,128)} %param.7) | data formatting | bytes 4194304 | tf_op args[0]
  10.2 2.4 %collective-permute-start.1 = (f32[16,1,4,128]{3,0,2,1:T(8,128)S(1)}, f32[16,1,4,128]{3,0,2,1:T(8,128)S(1)}, u32[]{:S(2)}, u32[]{:S(2)}) collective-permute-start(f32[16,1,4,128]{3,0,2,1:T(8,128)S(1)} %get-tuple-element.17), channel_id=1, source_target_pairs={{0,8},{8,16},{16,24},{1,9},{9,17},{17,25},{2,10},{10,18},{18,26},{... | collective-permute-start | bytes 98312 | tf_op jit(solution)/shard_map/ppermute | solution.py:14
  12.6 1.3 collective-permute-start
  14.0 1.2 constant_dynamic-update-slice_fusion.1
  15.2 2.6 %collective-permute-done = f32[16,1,4,128]{3,0,2,1:T(8,128)S(1)} collective-permute-done((f32[16,1,4,128]{3,0,2,1:T(8,128)S(1)}, f32[16,1,4,128]{3,0,2,1:T(8,128)S(1)}, u32[]{:S(2)}, u32[]{:S(2)}) %collective-permute-start) | collective-permute-done | bytes 32800 | tf_op jit(solution)/shard_map/ppermute | solution.py:17
  17.9 1.3 collective-permute-start.2
  19.2 4.6 %collective-permute-start.3 = (f32[16,66,1,128]{3,0,2,1:T(8,128)S(1)}, f32[16,66,1,128]{3,0,2,1:T(8,128)S(1)}, u32[]{:S(2)}, u32[]{:S(2)}) collective-permute-start(f32[16,66,1,128]{3,0,2,1:T(8,128)S(1)} %get-tuple-element.14), channel_id=1, source_target_pairs={{0,4},{1,5},{2,6},{3,7},{8,12},{9,13},{10,14},{11,15},{16,20},{17,... | collective-permute-start | bytes 1622024 | tf_op jit(solution)/shard_map/ppermute | solution.py:14
  23.8 9.5 %collective-permute-done.2 = f32[16,66,1,128]{3,0,2,1:T(8,128)S(1)} collective-permute-done((f32[16,66,1,128]{3,0,2,1:T(8,128)S(1)}, f32[16,66,1,128]{3,0,2,1:T(8,128)S(1)}, u32[]{:S(2)}, u32[]{:S(2)}) %collective-permute-start.2) | collective-permute-done | bytes 540704 | tf_op jit(solution)/shard_map/ppermute | solution.py:17
  33.3 1.8 collective-permute-done.3
  35.1 0.8 copy-done.8
  35.9 0.3 pad_maximum_fusion
  36.2 2.9 %fusion.12 = (f32[16,66,6,1]{3,0,2,1:T(8,128)}, f32[16,66,6,1]{3,0,2,1:T(8,128)S(1)}) fusion(f32[16,66,6,128]{3,0,2,1:T(8,128)S(1)} %pad_maximum_fusion), kind=kLoop, calls=%fused_computation.30 | loop fusion | bytes 101376 | tf_op jit(solution)/shard_map/slice | solution.py:17
  39.0 2.8 %copy.45 = f32[16,66,6,1]{1,0,3,2:T(8,128)S(1)} copy(f32[16,66,6,1]{3,0,2,1:T(8,128)} %get-tuple-element.12) | data formatting | bytes 50688 | tf_op jit(solution)/shard_map/slice | solution.py:17
  41.8 1.3 collective-permute-start.4
  43.1 2.2 %copy.47 = f32[16,66,6,1]{1,0,3,2:T(8,128)} copy(f32[16,66,6,1]{3,0,2,1:T(8,128)S(1)} %get-tuple-element.13) | data formatting | bytes 50688 | tf_op jit(solution)/shard_map/slice | solution.py:15
  45.3 5.2 %collective-permute-start.5 = (f32[16,66,6,1]{1,0,3,2:T(8,128)}, f32[16,66,6,1]{1,0,3,2:T(8,128)}, u32[]{:S(2)}, u32[]{:S(2)}) collective-permute-start(f32[16,66,6,1]{1,0,3,2:T(8,128)} %copy.47), channel_id=1, source_target_pairs={{0,1},{1,2},{2,3},{4,5},{5,6},{6,7},{8,9},{9,10},{10,11},{12,13},{... | collective-permute-start | bytes 76040 | tf_op jit(solution)/shard_map/ppermute | solution.py:14
  50.5 1.8 slice_bitcast_fusion.2
  52.2 2.6 %copy.46 = f32[16,66,6,1]{3,0,2,1:T(8,128)} copy(f32[16,66,6,1]{1,0,3,2:T(8,128)S(1)} %collective-permute-done.4) | data formatting | bytes 50688 | tf_op jit(solution)/shard_map/ppermute | solution.py:17
  54.9 3.6 %copy.48 = f32[16,66,6,1]{3,0,2,1:T(8,128)} copy(f32[16,66,6,1]{1,0,3,2:T(8,128)} %collective-permute-done.5) | data formatting | bytes 50688 | tf_op jit(solution)/shard_map/ppermute | solution.py:14
  58.5 10.6 %fusion.15 = (bf16[16,64,4,128]{3,0,2,1:T(8,128)(2,1)}, f32[16,64,4,128]{3,0,2,1:T(8,128)}) fusion(f32[16,64,4,128]{3,0,2,1:T(8,128)} %copy-done.4, f32[16,16]{1,0:T(8,128)S(1)} %copy-done.14, f32[64,4,128]{2,1,0:T(4,128)} %get-tuple-element.19, f32[64,4,128]{2,1,0:T(4,128)} %get-tuple-element.20, f32[64,4,128]{2,1,0:T(4,128)S(1)} %get-tuple-element.18, ...), kind=kOutput, calls=%fused_computation.33 | convolution fusion | flops 119537664 | bytes 11094593 | tf_op jit(solution)/shard_map/vw,wyzx->vyzx/dot_general | solution.py:41
  69.4 80.7 %all-gather.2.cloned.1.call-done = bf16[16,64,4,512]{3,0,2,1:T(8,128)(2,1)} async-done(((bf16[16,64,4,128]{3,0,2,1:T(8,128)(2,1)}), bf16[16,64,4,512]{3,0,2,1:T(8,128)(2,1)}) %all-gather.2.cloned.1.call-update) | async-done | bytes 4194320 | tf_op jit(solution)/shard_map/all_gather | solution.py:49
  150.1 6.8 %convolution_bitcast_fusion = f32[512,512]{1,0:T(8,128)} fusion(bf16[16,64,4,512]{3,0,2,1:T(8,128)(2,1)} %all-gather.2.cloned.1.call-done), kind=kOutput, calls=%fused_computation.18 | convolution fusion | flops 2147483648 | bytes 5242880 | tf_op jit(solution)/shard_map/dot_general | solution.py:54
  157.0 6.9 %fusion.7 = bf16[64,4,16,64]{3,0,1,2:T(8,128)(2,1)S(1)} fusion(bf16[16,64,4,512]{3,0,2,1:T(8,128)(2,1)} %all-gather.2.cloned.1.call-done, bf16[512,64]{0,1:T(8,128)(2,1)S(1)} %copy-done), kind=kOutput, calls=%fused_computation.17 | convolution fusion | flops 268697600 | bytes 4784128 | tf_op jit(solution)/shard_map/vyzx,xr->yzvr/dot_general | solution.py:62
  163.9 0.7 copy.54
  164.6 1.5 reshape.22
  166.1 3.5 %all-to-all-start = ((bf16[64,4,1024]{2,0,1:T(8,128)(2,1)}), bf16[64,4,1024]{2,0,1:T(8,128)(2,1)S(1)}, u32[]{:S(2)}, u32[]{:S(2)}) async-start(bf16[64,4,1024]{2,0,1:T(8,128)(2,1)} %reshape.22), calls=%async_computation.1 | async-start | bytes 1048576 | tf_op jit(solution)/shard_map/all_to_all | solution.py:66
  169.6 2.1 %copy.55 = f32[16,64,4,128]{3,2,1,0:T(4,128)} copy(f32[16,64,4,128]{3,0,2,1:T(8,128)S(1)} %copy-done.5) | data formatting | bytes 4194304
  171.7 8.1 %all-to-all-done = bf16[64,4,1024]{2,0,1:T(8,128)(2,1)S(1)} async-done(((bf16[64,4,1024]{2,0,1:T(8,128)(2,1)}), bf16[64,4,1024]{2,0,1:T(8,128)(2,1)S(1)}, u32[]{:S(2)}, u32[]{:S(2)}) %all-to-all-start) | async-done | bytes 524320 | tf_op jit(solution)/shard_map/all_to_all | solution.py:66
  179.9 0.3 convolution_multiply_fusion
  180.2 1.0 convolution_bitcast_fusion.1
  181.2 10.1 %reduce-scatter.2.cloned.1.call-done = f32[64,512]{1,0:T(8,128)} async-done(((f32[512,512]{1,0:T(8,128)}), f32[64,512]{1,0:T(8,128)}) %reduce-scatter.2.cloned.1.call-update) | async-done | bytes 131088 | tf_op jit(solution)/shard_map/reduce_scatter | solution.py:53
  191.3 1.6 broadcast_multiply_fusion
  (42 shorter events, 0.5 us)
Async XLA Ops:
  7.2 149.8 %copy-start = (bf16[512,64]{0,1:T(8,128)(2,1)S(1)}, bf16[512,64]{0,1:T(8,128)(2,1)}, u32[]{:S(2)}) copy-start(bf16[512,64]{0,1:T(8,128)(2,1)} %param.12) | copy-start | bytes 196612
  7.2 6.8 %copy-start.1 = (f32[16,64,4,128]{3,2,1,0:T(4,128)S(1)}, f32[16,64,4,128]{3,2,1,0:T(4,128)}, u32[]{:S(2)}) copy-start(f32[16,64,4,128]{3,2,1,0:T(4,128)} %param.7) | copy-start | bytes 6291460
  7.2 142.9 %all-gather.2.cloned.1.call-start = ((), (), s32[]{:S(2)}) async-start(), calls=%async_computation.2 | async-start | bytes 5242880 | tf_op jit(solution)/shard_map/all_gather | solution.py:49
  10.2 5.0 %copy-start.4 = (f32[16,64,4,128]{3,0,2,1:T(8,128)}, f32[16,64,4,128]{3,0,2,1:T(8,128)S(1)}, u32[]{:S(2)}) copy-start(f32[16,64,4,128]{3,0,2,1:T(8,128)S(1)} %copy.52) | copy-start | bytes 6291460
  10.2 3.7 %collective-permute-start.1 = (f32[16,1,4,128]{3,0,2,1:T(8,128)S(1)}, f32[16,1,4,128]{3,0,2,1:T(8,128)S(1)}, u32[]{:S(2)}, u32[]{:S(2)}) collective-permute-start(f32[16,1,4,128]{3,0,2,1:T(8,128)S(1)} %get-tuple-element.17), channel_id=1, source_target_pairs={{0,8},{8,16},{16,24},{1,9},{9,17},{17,25},{2,10},{10,18},{18,26},{... | collective-permute-start | bytes 98312 | tf_op jit(solution)/shard_map/ppermute | solution.py:14
  12.6 5.2 %collective-permute-start = (f32[16,1,4,128]{3,0,2,1:T(8,128)S(1)}, f32[16,1,4,128]{3,0,2,1:T(8,128)S(1)}, u32[]{:S(2)}, u32[]{:S(2)}) collective-permute-start(f32[16,1,4,128]{3,0,2,1:T(8,128)S(1)} %get-tuple-element.16), channel_id=1, source_target_pairs={{8,0},{16,8},{24,16},{9,1},{17,9},{25,17},{10,2},{18,10},{26,18},{... | collective-permute-start | bytes 98312 | tf_op jit(solution)/shard_map/ppermute | solution.py:17
  13.9 1.3 copy-start.11
  17.8 15.5 %copy-start.13 = (f32[16,1,4,128]{3,0,2,1:T(8,128)}, f32[16,1,4,128]{3,0,2,1:T(8,128)S(1)}, u32[]{:S(2)}) copy-start(f32[16,1,4,128]{3,0,2,1:T(8,128)S(1)} %collective-permute-done) | copy-start | bytes 98308
  17.8 17.2 %copy-start.2 = (f32[16,66,4,128]{3,0,2,1:T(8,128)}, f32[16,66,4,128]{3,0,2,1:T(8,128)S(1)}, u32[]{:S(2)}) copy-start(f32[16,66,4,128]{3,0,2,1:T(8,128)S(1)} %constant_dynamic-update-slice_fusion) | copy-start | bytes 6488068
  17.9 15.4 %collective-permute-start.2 = (f32[16,66,1,128]{3,0,2,1:T(8,128)S(1)}, f32[16,66,1,128]{3,0,2,1:T(8,128)S(1)}, u32[]{:S(2)}, u32[]{:S(2)}) collective-permute-start(f32[16,66,1,128]{3,0,2,1:T(8,128)S(1)} %get-tuple-element.15), channel_id=1, source_target_pairs={{4,0},{5,1},{6,2},{7,3},{12,8},{13,9},{14,10},{15,11},{20,16},{21,... | collective-permute-start | bytes 1622024 | tf_op jit(solution)/shard_map/ppermute | solution.py:17
  19.2 15.9 %collective-permute-start.3 = (f32[16,66,1,128]{3,0,2,1:T(8,128)S(1)}, f32[16,66,1,128]{3,0,2,1:T(8,128)S(1)}, u32[]{:S(2)}, u32[]{:S(2)}) collective-permute-start(f32[16,66,1,128]{3,0,2,1:T(8,128)S(1)} %get-tuple-element.14), channel_id=1, source_target_pairs={{0,4},{1,5},{2,6},{3,7},{8,12},{9,13},{10,14},{11,15},{16,20},{17,... | collective-permute-start | bytes 1622024 | tf_op jit(solution)/shard_map/ppermute | solution.py:14
  33.3 1.8 copy-start.6
  35.1 0.8 copy-start.8
  41.8 10.4 %collective-permute-start.4 = (f32[16,66,6,1]{1,0,3,2:T(8,128)S(1)}, f32[16,66,6,1]{1,0,3,2:T(8,128)S(1)}, u32[]{:S(2)}, u32[]{:S(2)}) collective-permute-start(f32[16,66,6,1]{1,0,3,2:T(8,128)S(1)} %copy.45), channel_id=1, source_target_pairs={{1,0},{2,1},{3,2},{5,4},{6,5},{7,6},{9,8},{10,9},{11,10},{13,12},{... | collective-permute-start | bytes 76040 | tf_op jit(solution)/shard_map/ppermute | solution.py:17
  45.3 9.6 %collective-permute-start.5 = (f32[16,66,6,1]{1,0,3,2:T(8,128)}, f32[16,66,6,1]{1,0,3,2:T(8,128)}, u32[]{:S(2)}, u32[]{:S(2)}) collective-permute-start(f32[16,66,6,1]{1,0,3,2:T(8,128)} %copy.47), channel_id=1, source_target_pairs={{0,1},{1,2},{2,3},{4,5},{5,6},{6,7},{8,9},{9,10},{10,11},{12,13},{... | collective-permute-start | bytes 76040 | tf_op jit(solution)/shard_map/ppermute | solution.py:14
  54.9 3.6 %copy-start.3 = (f32[16,66,4,128]{3,0,2,1:T(8,128)S(1)}, f32[16,66,4,128]{3,0,2,1:T(8,128)}, u32[]{:S(2)}) copy-start(f32[16,66,4,128]{3,0,2,1:T(8,128)} %copy-done.2) | copy-start | bytes 6488068
  54.9 3.6 %copy-start.7 = (f32[16,66,1,128]{3,0,2,1:T(8,128)S(1)}, f32[16,66,1,128]{3,0,2,1:T(8,128)}, u32[]{:S(2)}) copy-start(f32[16,66,1,128]{3,0,2,1:T(8,128)} %copy-done.6) | copy-start | bytes 1622020
  54.9 3.6 %copy-start.9 = (f32[16,66,1,128]{3,0,2,1:T(8,128)S(1)}, f32[16,66,1,128]{3,0,2,1:T(8,128)}, u32[]{:S(2)}) copy-start(f32[16,66,1,128]{3,0,2,1:T(8,128)} %copy-done.8) | copy-start | bytes 1622020
  54.9 3.6 %copy-start.12 = (f32[16,1,4,128]{3,0,2,1:T(8,128)S(1)}, f32[16,1,4,128]{3,0,2,1:T(8,128)}, u32[]{:S(2)}) copy-start(f32[16,1,4,128]{3,0,2,1:T(8,128)} %copy-done.11) | copy-start | bytes 98308
  54.9 3.6 %copy-start.14 = (f32[16,16]{1,0:T(8,128)S(1)}, f32[16,16]{1,0:T(8,128)}, u32[]{:S(2)}) copy-start(f32[16,16]{1,0:T(8,128)} %param.11) | copy-start | bytes 3076
  54.9 3.6 %copy-start.15 = (f32[16]{0:T(128)S(1)}, f32[16]{0:T(128)}, u32[]{:S(2)}) copy-start(f32[16]{0:T(128)} %param.10) | copy-start | bytes 196
  69.1 122.2 %reduce-scatter.2.cloned.1.call-start = ((), (), s32[]{:S(2)}) async-start(), calls=%async_computation.3 | async-start | bytes 1179648 | tf_op jit(solution)/shard_map/reduce_scatter | solution.py:53
  163.9 5.7 %copy-start.5 = (f32[16,64,4,128]{3,0,2,1:T(8,128)S(1)}, f32[16,64,4,128]{3,0,2,1:T(8,128)}, u32[]{:S(2)}) copy-start(f32[16,64,4,128]{3,0,2,1:T(8,128)} %get-tuple-element.22) | copy-start | bytes 6291460
  166.1 13.8 %all-to-all-start = ((bf16[64,4,1024]{2,0,1:T(8,128)(2,1)}), bf16[64,4,1024]{2,0,1:T(8,128)(2,1)S(1)}, u32[]{:S(2)}, u32[]{:S(2)}) async-start(bf16[64,4,1024]{2,0,1:T(8,128)(2,1)} %reshape.22), calls=%async_computation.1 | async-start | bytes 1048576 | tf_op jit(solution)/shard_map/all_to_all | solution.py:66
  169.6 10.6 %copy-start.10 = (f32[256,64]{0,1:T(8,128)S(1)}, f32[256,64]{0,1:T(8,128)}, u32[]{:S(2)}) copy-start(f32[256,64]{0,1:T(8,128)} %param.13) | copy-start | bytes 196612
Sparse Core Ops, SparseCore 0:
  69.3 80.7 all-gather.1
  157.1 34.1 reduce-scatter.1
where the time goes:
time: 200 us
  waiting for transfers between devices  113 us (56%)
  matrix products  25.7 us (13%)
  local copies, waits for them, and re-layouts  25.3 us (13%)
  starting transfers between devices  19.8 us (10%)
  between operations  14.3 us (7%)
    all_gather x1, waiting for transfers between devices, shards(): gathered = lax.all_gather(snapshot, 'ga', axis=3, tiled=True)  80.7 us
    ppermute x3, starting transfers between devices, with_halo(): lax.ppermute(lax.slice_in_dim(block, block.shape[dim] - width, None, axis...  12.2 us
    ppermute x3, waiting for transfers between devices, with_halo(): lax.ppermute(lax.slice_in_dim(block, 0, width, axis=dim), axis, backward)  12.1 us
    dot_general x1, matrix products, shards(): jnp.einsum('vw,wyzx->vyzx', reaction, fields, precision=lax.Precision.HIG...  10.6 us
    reduce_scatter x1, waiting for transfers between devices, shards(): lax.psum_scatter(lax.dot_general(unfolded, unfolded, (((0,), (0,)), ((),...  10.1 us
    all_to_all x1, waiting for transfers between devices, shards(): lax.all_to_all(projected, 'gy', split_axis=1, concat_axis=0, tiled=True)  8.14 us
    unnamed x36, local copies, waits for them, and re-layouts  7.19 us
    dot_general x1, matrix products, shards(): jnp.einsum('vyzx,xr->yzvr', gathered, x_factor, preferred_element_type=jn...  6.91 us
  transfers between devices with their start and end apart: 9, of which 6 were waited for; matrix products, arithmetic and copies ran while one was open for 10% of the time, Pallas kernels for 0%

commit v1 on v0

--- a/solution.py
+++ b/solution.py
@@ -46,7 +46,8 @@
     snapshot = new_fields.astype(jnp.bfloat16)
     devices = lax.axis_size("gy") * lax.axis_size("gz")
     rank_x = x_factor.shape[1]
-    gathered = lax.all_gather(snapshot, "ga", axis=3, tiled=True)
+    repeated = jnp.stack([snapshot] * lax.axis_size("ga"))
+    gathered = jnp.concatenate(lax.all_to_all(repeated, "ga", 0, 0), axis=3)
     variables, y_cells, z_cells, x_cells = gathered.shape
     unfolded = gathered.reshape(variables * y_cells * z_cells, x_cells)
     cell_count = float(variables * y_cells * z_cells * devices)

time: 200 us -> 224 us (1.12)
  blocking collectives: 0 us -> 97.3 us
  waiting for transfers between devices: 113 us -> 21.9 us
  local copies, waits for them, and re-layouts: 25.3 us -> 50.2 us
  matrix products: 25.7 us -> 18.3 us
    all_to_all x0 -> x1, blocking collectives: none -> 97.3 us  [shards(): gathered = jnp.concatenate(lax.all_to_all(repeated, 'ga', 0, 0), axis=3)]
    all_gather x1 -> x0, waiting for transfers between devices: 80.7 us -> none  [shards(): gathered = lax.all_gather(snapshot, 'ga', axis=3, tiled=True)]
    reshape x0 -> x3, local copies, waits for them, and re-layouts: none -> 22.3 us  [shards(): gathered = jnp.concatenate(lax.all_to_all(repeated, 'ga', 0, 0), axis=3)]
    reduce_scatter x1, waiting for transfers between devices: 10.1 us -> 0.01 us  [shards(): lax.psum_scatter(lax.dot_general(unfolded, unfolded, (((0,), (0,)), ((),...]
    dot_general x1, matrix products: 6.83 us -> 3.34 us  [shards(): lax.dot_general(unfolded, unfolded, (((0,), (0,)), ((), ())), preferred_e...]
    dot_general x1, matrix products: 6.91 us -> 3.42 us  [shards(): jnp.einsum('vyzx,xr->yzvr', gathered, x_factor, preferred_element_type=jn...]
    unnamed x36 -> x38, local copies, waits for them, and re-layouts: 7.19 us -> 7.2 us
  transfers between devices with their start and end apart: 9 -> 8, of which waited for: 6 -> 4; matrix products, arithmetic and copies ran while one was open for 10% -> 15% of each run, Pallas kernels for 0% -> 0%
where the time goes in v1:
time: 224 us; the launch traced here: 223 us
  blocking collectives  97.3 us (43%)
  local copies, waits for them, and re-layouts  50.2 us (22%)
  waiting for transfers between devices  21.9 us (10%)
  starting transfers between devices  19.5 us (9%)
  matrix products  18.3 us (8%)
  between operations  14.3 us (6%)
    all_to_all x1, blocking collectives, shards(): gathered = jnp.concatenate(lax.all_to_all(repeated, 'ga', 0, 0), axis=3)  97.3 us
    reshape x3, local copies, waits for them, and re-layouts, shards(): gathered = jnp.concatenate(lax.all_to_all(repeated, 'ga', 0, 0), axis=3)  22.3 us
    ppermute x3, starting transfers between devices, with_halo(): lax.ppermute(lax.slice_in_dim(block, block.shape[dim] - width, None, axis...  12.2 us
    ppermute x3, waiting for transfers between devices, with_halo(): lax.ppermute(lax.slice_in_dim(block, 0, width, axis=dim), axis, backward)  12.1 us
    dot_general x1, matrix products, shards(): jnp.einsum('vw,wyzx->vyzx', reaction, fields, precision=lax.Precision.HIG...  10.2 us
    all_to_all x1, waiting for transfers between devices, shards(): lax.all_to_all(projected, 'gy', split_axis=1, concat_axis=0, tiled=True)  8.03 us
    unnamed x38, local copies, waits for them, and re-layouts  7.2 us
    slice x3, local copies, waits for them, and re-layouts, with_halo(): lax.slice_in_dim(block, 0, width, axis=dim)  5.66 us
  transfers between devices with their start and end apart: 8, of which 4 were waited for; matrix products, arithmetic and copies ran while one was open for 15% of the time, Pallas kernels for 0%

profile of v1, /device:TPU:0, one launch (start us, length us, event | category | flops | bytes accessed | tf_op | source)
XLA Modules:
  0.0 223.4 jit_solution(16350344933387058608)
XLA Ops:
  7.2 3.0 %copy.49 = f32[16,64,4,128]{3,0,2,1:T(8,128)S(1)} copy(f32[16,64,4,128]{3,2,1,0:T(4,128)} %param.7) | data formatting | bytes 4194304 | tf_op args[0]
  10.2 2.4 %collective-permute-start.1 = (f32[16,1,4,128]{3,0,2,1:T(8,128)S(1)}, f32[16,1,4,128]{3,0,2,1:T(8,128)S(1)}, u32[]{:S(2)}, u32[]{:S(2)}) collective-permute-start(f32[16,1,4,128]{3,0,2,1:T(8,128)S(1)} %get-tuple-element.17), channel_id=1, source_target_pairs={{0,8},{8,16},{16,24},{1,9},{9,17},{17,25},{2,10},{10,18},{18,26},{... | collective-permute-start | bytes 98312 | tf_op jit(solution)/shard_map/ppermute | solution.py:14
  12.6 1.3 collective-permute-start
  14.0 1.2 constant_dynamic-update-slice_fusion.1
  15.2 2.6 %collective-permute-done = f32[16,1,4,128]{3,0,2,1:T(8,128)S(1)} collective-permute-done((f32[16,1,4,128]{3,0,2,1:T(8,128)S(1)}, f32[16,1,4,128]{3,0,2,1:T(8,128)S(1)}, u32[]{:S(2)}, u32[]{:S(2)}) %collective-permute-start) | collective-permute-done | bytes 32800 | tf_op jit(solution)/shard_map/ppermute | solution.py:17
  17.9 1.3 collective-permute-start.2
  19.2 4.6 %collective-permute-start.3 = (f32[16,66,1,128]{3,0,2,1:T(8,128)S(1)}, f32[16,66,1,128]{3,0,2,1:T(8,128)S(1)}, u32[]{:S(2)}, u32[]{:S(2)}) collective-permute-start(f32[16,66,1,128]{3,0,2,1:T(8,128)S(1)} %get-tuple-element.14), channel_id=1, source_target_pairs={{0,4},{1,5},{2,6},{3,7},{8,12},{9,13},{10,14},{11,15},{16,20},{17,... | collective-permute-start | bytes 1622024 | tf_op jit(solution)/shard_map/ppermute | solution.py:14
  23.8 9.5 %collective-permute-done.2 = f32[16,66,1,128]{3,0,2,1:T(8,128)S(1)} collective-permute-done((f32[16,66,1,128]{3,0,2,1:T(8,128)S(1)}, f32[16,66,1,128]{3,0,2,1:T(8,128)S(1)}, u32[]{:S(2)}, u32[]{:S(2)}) %collective-permute-start.2) | collective-permute-done | bytes 540704 | tf_op jit(solution)/shard_map/ppermute | solution.py:17
  33.3 1.8 collective-permute-done.3
  35.1 0.8 copy-done.9
  36.2 2.9 %fusion.8 = (f32[16,66,6,1]{3,0,2,1:T(8,128)}, f32[16,66,6,1]{3,0,2,1:T(8,128)S(1)}) fusion(f32[16,66,6,128]{3,0,2,1:T(8,128)S(1)} %pad_maximum_fusion), kind=kLoop, calls=%fused_computation.30 | loop fusion | bytes 101376 | tf_op jit(solution)/shard_map/slice | solution.py:17
  39.0 2.8 %copy.42 = f32[16,66,6,1]{1,0,3,2:T(8,128)S(1)} copy(f32[16,66,6,1]{3,0,2,1:T(8,128)} %get-tuple-element.12) | data formatting | bytes 50688 | tf_op jit(solution)/shard_map/slice | solution.py:17
  41.8 1.3 collective-permute-start.4
  43.1 2.2 copy.44
  45.3 5.2 %collective-permute-start.5 = (f32[16,66,6,1]{1,0,3,2:T(8,128)}, f32[16,66,6,1]{1,0,3,2:T(8,128)}, u32[]{:S(2)}, u32[]{:S(2)}) collective-permute-start(f32[16,66,6,1]{1,0,3,2:T(8,128)} %copy.44), channel_id=1, source_target_pairs={{0,1},{1,2},{2,3},{4,5},{5,6},{6,7},{8,9},{9,10},{10,11},{12,13},{... | collective-permute-start | bytes 76040 | tf_op jit(solution)/shard_map/ppermute | solution.py:14
  50.5 1.7 slice_bitcast_fusion.2
  52.2 2.8 %copy.43 = f32[16,66,6,1]{3,0,2,1:T(8,128)} copy(f32[16,66,6,1]{1,0,3,2:T(8,128)S(1)} %collective-permute-done.4) | data formatting | bytes 50688 | tf_op jit(solution)/shard_map/ppermute | solution.py:17
  55.1 3.5 %copy.45 = f32[16,66,6,1]{3,0,2,1:T(8,128)} copy(f32[16,66,6,1]{1,0,3,2:T(8,128)} %collective-permute-done.5) | data formatting | bytes 50688 | tf_op jit(solution)/shard_map/ppermute | solution.py:14
  58.6 10.2 %fusion.11 = (bf16[16,64,4,128]{3,0,2,1:T(8,128)(2,1)S(1)}, f32[16,64,4,128]{3,0,2,1:T(8,128)}) fusion(f32[16,64,4,128]{3,0,2,1:T(8,128)} %copy-done.5, f32[16,16]{1,0:T(8,128)S(1)} %copy-done.15, f32[64,4,128]{2,1,0:T(4,128)} %get-tuple-element.19, f32[64,4,128]{2,1,0:T(4,128)} %get-tuple-element.20, f32[64,4,128]{2,1,0:T(4,128)S(1)} %get-tuple-element.18, ...), kind=kOutput, calls=%fused_computation.33 | convolution fusion | flops 119537664 | bytes 11094593 | tf_op jit(solution)/shard_map/vw,wyzx->vyzx/dot_general | solution.py:41
  69.3 2.0 stack.2
  71.3 97.3 %all_to_all.20 = bf16[4,16,64,4,128]{4,3,2,1,0:T(4,128)(2,1)S(1)} all-to-all(bf16[4,16,64,4,128]{4,3,2,1,0:T(4,128)(2,1)S(1)} %stack.2), channel_id=1, replica_groups=mesh['gy'=4,'gz'=2,'ga'=4] {'ga'}, dimensions={0} | all-to-all | bytes 8388608 | tf_op jit(solution)/shard_map/all_to_all | solution.py:50
  168.6 5.8 %copy.51 = bf16[16,64,4,4,128]{4,3,2,1,0:T(4,128)(2,1)S(1)} copy(bf16[16,64,4,4,128]{4,2,1,0,3:T(4,128)(2,1)S(1)} %bitcast.45) | data formatting | bytes 8388608 | tf_op jit(solution)/shard_map/reshape | solution.py:50
  174.5 3.3 %fusion = f32[512,512]{1,0:T(8,128)} fusion(bf16[512,8,4,128]{3,2,1,0:T(4,128)(2,1)S(1)} %bitcast.48), kind=kOutput, calls=%fused_computation | convolution fusion | flops 2147483648 | bytes 5242880 | tf_op jit(solution)/shard_map/dot_general | solution.py:55
  177.9 9.2 %copy.52 = bf16[16,64,4,4,128]{4,3,1,2,0:T(4,128)(2,1)} copy(bf16[16,64,4,4,128]{4,2,1,0,3:T(4,128)(2,1)} %bitcast.46) | data formatting | bytes 8388608 | tf_op jit(solution)/shard_map/reshape | solution.py:50
  187.1 7.2 %reshape.30 = bf16[16,64,4,512]{3,1,2,0:T(8,128)(2,1)} reshape(bf16[16,64,4,4,128]{4,3,1,2,0:T(4,128)(2,1)} %copy.52) | data formatting | bytes 8388608 | tf_op jit(solution)/shard_map/reshape | solution.py:50
  194.3 3.4 %fusion.5 = bf16[64,4,16,64]{3,0,1,2:T(8,128)(2,1)S(1)} fusion(bf16[16,64,4,512]{3,1,2,0:T(8,128)(2,1)} %reshape.30, bf16[512,64]{0,1:T(8,128)(2,1)S(1)} %copy-done), kind=kOutput, calls=%fused_computation.18 | convolution fusion | flops 268697600 | bytes 4784128 | tf_op jit(solution)/shard_map/vyzx,xr->yzvr/dot_general | solution.py:63
  198.4 1.5 reshape.31
  200.0 3.5 %all-to-all-start.1 = ((bf16[64,4,1024]{2,0,1:T(8,128)(2,1)}), bf16[64,4,1024]{2,0,1:T(8,128)(2,1)S(1)}, u32[]{:S(2)}, u32[]{:S(2)}) async-start(bf16[64,4,1024]{2,0,1:T(8,128)(2,1)} %reshape.31), calls=%async_computation.2 | async-start | bytes 1048576 | tf_op jit(solution)/shard_map/all_to_all | solution.py:67
  203.5 2.1 copy.54
  205.6 8.0 %all-to-all-done.1 = bf16[64,4,1024]{2,0,1:T(8,128)(2,1)S(1)} async-done(((bf16[64,4,1024]{2,0,1:T(8,128)(2,1)}), bf16[64,4,1024]{2,0,1:T(8,128)(2,1)S(1)}, u32[]{:S(2)}, u32[]{:S(2)}) %all-to-all-start.1) | async-done | bytes 524320 | tf_op jit(solution)/shard_map/all_to_all | solution.py:67
  214.0 1.0 convolution_bitcast_fusion
  215.0 1.6 broadcast_multiply_fusion
  (47 shorter events, 2.0 us)
Async XLA Ops:
  7.2 187.1 %copy-start = (bf16[512,64]{0,1:T(8,128)(2,1)S(1)}, bf16[512,64]{0,1:T(8,128)(2,1)}, u32[]{:S(2)}) copy-start(bf16[512,64]{0,1:T(8,128)(2,1)} %param.12) | copy-start | bytes 196612
  7.2 6.8 %copy-start.2 = (f32[16,64,4,128]{3,2,1,0:T(4,128)S(1)}, f32[16,64,4,128]{3,2,1,0:T(4,128)}, u32[]{:S(2)}) copy-start(f32[16,64,4,128]{3,2,1,0:T(4,128)} %param.7) | copy-start | bytes 6291460
  7.2 207.8 %reduce-scatter.2.cloned.1.call-start = ((), (), s32[]{:S(2)}) async-start(), calls=%async_computation.3 | async-start | bytes 1179648 | tf_op jit(solution)/shard_map/reduce_scatter | solution.py:54
  10.2 5.0 %copy-start.5 = (f32[16,64,4,128]{3,0,2,1:T(8,128)}, f32[16,64,4,128]{3,0,2,1:T(8,128)S(1)}, u32[]{:S(2)}) copy-start(f32[16,64,4,128]{3,0,2,1:T(8,128)S(1)} %copy.49) | copy-start | bytes 6291460
  10.2 3.7 %collective-permute-start.1 = (f32[16,1,4,128]{3,0,2,1:T(8,128)S(1)}, f32[16,1,4,128]{3,0,2,1:T(8,128)S(1)}, u32[]{:S(2)}, u32[]{:S(2)}) collective-permute-start(f32[16,1,4,128]{3,0,2,1:T(8,128)S(1)} %get-tuple-element.17), channel_id=1, source_target_pairs={{0,8},{8,16},{16,24},{1,9},{9,17},{17,25},{2,10},{10,18},{18,26},{... | collective-permute-start | bytes 98312 | tf_op jit(solution)/shard_map/ppermute | solution.py:14
  12.6 5.2 %collective-permute-start = (f32[16,1,4,128]{3,0,2,1:T(8,128)S(1)}, f32[16,1,4,128]{3,0,2,1:T(8,128)S(1)}, u32[]{:S(2)}, u32[]{:S(2)}) collective-permute-start(f32[16,1,4,128]{3,0,2,1:T(8,128)S(1)} %get-tuple-element.16), channel_id=1, source_target_pairs={{8,0},{16,8},{24,16},{9,1},{17,9},{25,17},{10,2},{18,10},{26,18},{... | collective-permute-start | bytes 98312 | tf_op jit(solution)/shard_map/ppermute | solution.py:17
  13.9 1.3 copy-start.12
  17.8 15.5 %copy-start.14 = (f32[16,1,4,128]{3,0,2,1:T(8,128)}, f32[16,1,4,128]{3,0,2,1:T(8,128)S(1)}, u32[]{:S(2)}) copy-start(f32[16,1,4,128]{3,0,2,1:T(8,128)S(1)} %collective-permute-done) | copy-start | bytes 98308
  17.8 17.2 %copy-start.3 = (f32[16,66,4,128]{3,0,2,1:T(8,128)}, f32[16,66,4,128]{3,0,2,1:T(8,128)S(1)}, u32[]{:S(2)}) copy-start(f32[16,66,4,128]{3,0,2,1:T(8,128)S(1)} %constant_dynamic-update-slice_fusion) | copy-start | bytes 6488068
  17.9 15.4 %collective-permute-start.2 = (f32[16,66,1,128]{3,0,2,1:T(8,128)S(1)}, f32[16,66,1,128]{3,0,2,1:T(8,128)S(1)}, u32[]{:S(2)}, u32[]{:S(2)}) collective-permute-start(f32[16,66,1,128]{3,0,2,1:T(8,128)S(1)} %get-tuple-element.15), channel_id=1, source_target_pairs={{4,0},{5,1},{6,2},{7,3},{12,8},{13,9},{14,10},{15,11},{20,16},{21,... | collective-permute-start | bytes 1622024 | tf_op jit(solution)/shard_map/ppermute | solution.py:17
  19.2 15.9 %collective-permute-start.3 = (f32[16,66,1,128]{3,0,2,1:T(8,128)S(1)}, f32[16,66,1,128]{3,0,2,1:T(8,128)S(1)}, u32[]{:S(2)}, u32[]{:S(2)}) collective-permute-start(f32[16,66,1,128]{3,0,2,1:T(8,128)S(1)} %get-tuple-element.14), channel_id=1, source_target_pairs={{0,4},{1,5},{2,6},{3,7},{8,12},{9,13},{10,14},{11,15},{16,20},{17,... | collective-permute-start | bytes 1622024 | tf_op jit(solution)/shard_map/ppermute | solution.py:14
  33.3 1.8 copy-start.7
  35.1 0.8 copy-start.9
  41.8 10.4 %collective-permute-start.4 = (f32[16,66,6,1]{1,0,3,2:T(8,128)S(1)}, f32[16,66,6,1]{1,0,3,2:T(8,128)S(1)}, u32[]{:S(2)}, u32[]{:S(2)}) collective-permute-start(f32[16,66,6,1]{1,0,3,2:T(8,128)S(1)} %copy.42), channel_id=1, source_target_pairs={{1,0},{2,1},{3,2},{5,4},{6,5},{7,6},{9,8},{10,9},{11,10},{13,12},{... | collective-permute-start | bytes 76040 | tf_op jit(solution)/shard_map/ppermute | solution.py:17
  45.3 9.7 %collective-permute-start.5 = (f32[16,66,6,1]{1,0,3,2:T(8,128)}, f32[16,66,6,1]{1,0,3,2:T(8,128)}, u32[]{:S(2)}, u32[]{:S(2)}) collective-permute-start(f32[16,66,6,1]{1,0,3,2:T(8,128)} %copy.44), channel_id=1, source_target_pairs={{0,1},{1,2},{2,3},{4,5},{5,6},{6,7},{8,9},{9,10},{10,11},{12,13},{... | collective-permute-start | bytes 76040 | tf_op jit(solution)/shard_map/ppermute | solution.py:14
  55.0 3.5 %copy-start.4 = (f32[16,66,4,128]{3,0,2,1:T(8,128)S(1)}, f32[16,66,4,128]{3,0,2,1:T(8,128)}, u32[]{:S(2)}) copy-start(f32[16,66,4,128]{3,0,2,1:T(8,128)} %copy-done.3) | copy-start | bytes 6488068
  55.0 3.5 %copy-start.8 = (f32[16,66,1,128]{3,0,2,1:T(8,128)S(1)}, f32[16,66,1,128]{3,0,2,1:T(8,128)}, u32[]{:S(2)}) copy-start(f32[16,66,1,128]{3,0,2,1:T(8,128)} %copy-done.7) | copy-start | bytes 1622020
  55.0 3.5 %copy-start.10 = (f32[16,66,1,128]{3,0,2,1:T(8,128)S(1)}, f32[16,66,1,128]{3,0,2,1:T(8,128)}, u32[]{:S(2)}) copy-start(f32[16,66,1,128]{3,0,2,1:T(8,128)} %copy-done.9) | copy-start | bytes 1622020
  55.0 3.5 %copy-start.13 = (f32[16,1,4,128]{3,0,2,1:T(8,128)S(1)}, f32[16,1,4,128]{3,0,2,1:T(8,128)}, u32[]{:S(2)}) copy-start(f32[16,1,4,128]{3,0,2,1:T(8,128)} %copy-done.12) | copy-start | bytes 98308
  55.0 3.6 %copy-start.15 = (f32[16,16]{1,0:T(8,128)S(1)}, f32[16,16]{1,0:T(8,128)}, u32[]{:S(2)}) copy-start(f32[16,16]{1,0:T(8,128)} %param.11) | copy-start | bytes 3076
  55.0 3.5 %copy-start.16 = (f32[16]{0:T(128)S(1)}, f32[16]{0:T(128)}, u32[]{:S(2)}) copy-start(f32[16]{0:T(128)} %param.10) | copy-start | bytes 196
  168.6 5.8 %copy-start.1 = (bf16[4,16,64,4,128]{4,3,2,1,0:T(4,128)(2,1)}, bf16[4,16,64,4,128]{4,3,2,1,0:T(4,128)(2,1)S(1)}, u32[]{:S(2)}) copy-start(bf16[4,16,64,4,128]{4,3,2,1,0:T(4,128)(2,1)S(1)} %all_to_all.20) | copy-start | bytes 12582916
  197.7 5.7 %copy-start.6 = (f32[16,64,4,128]{3,0,2,1:T(8,128)S(1)}, f32[16,64,4,128]{3,0,2,1:T(8,128)}, u32[]{:S(2)}) copy-start(f32[16,64,4,128]{3,0,2,1:T(8,128)} %get-tuple-element.22) | copy-start | bytes 6291460
  200.0 13.7 %all-to-all-start.1 = ((bf16[64,4,1024]{2,0,1:T(8,128)(2,1)}), bf16[64,4,1024]{2,0,1:T(8,128)(2,1)S(1)}, u32[]{:S(2)}, u32[]{:S(2)}) async-start(bf16[64,4,1024]{2,0,1:T(8,128)(2,1)} %reshape.31), calls=%async_computation.2 | async-start | bytes 1048576 | tf_op jit(solution)/shard_map/all_to_all | solution.py:67
  203.5 10.5 %copy-start.11 = (f32[256,64]{0,1:T(8,128)S(1)}, f32[256,64]{0,1:T(8,128)}, u32[]{:S(2)}) copy-start(f32[256,64]{0,1:T(8,128)} %param.13) | copy-start | bytes 196612
Sparse Core Ops, SparseCore 0:
  178.0 36.0 reduce-scatter.1
